TPU v7x, 128 devices: a whole 4x4x4 slice. The times are simulated.
128 devices in a mesh: grp: 8 (over x, core), tp: 16 (over z, y).
Axes of the slice: x: 4, y: 4, z: 4, core: 2. Of those that a mesh axis runs over, the one named last changes fastest.
Arguments:
- hidden_states: bfloat16 [2048, 8192], P('grp', 'tp'), may hold values from -6 to 6
- norm_gain: float32 [8192], replicated, may hold values from 0.5 to 1.5
- w_query: bfloat16 [8192, 8192], P(None, 'tp'), may hold values from -0.0625 to 0.0625
- w_key: bfloat16 [8192, 1024], P(None, 'tp'), may hold values from -0.0625 to 0.0625
- w_value: bfloat16 [8192, 1024], P(None, 'tp'), may hold values from -0.0625 to 0.0625
- cache: bfloat16 [16384, 2048], P('grp', 'tp'), may hold values from -82 to 82
- w_out: bfloat16 [8192, 8192], P('tp'), may hold values from -6 to 6
Outputs:
- mixed: bfloat16 [2048, 8192], P('grp', 'tp')
All inputs are finite; a program needn't handle non-finite values.
Results may differ from a plain program's by a relative error of at most 0.03.
Values may be sent and summed in bfloat16 or wider, within the bound.
A program may use at most 128 MiB of HBM per device.

v0:
```python
import math
import jax
import jax.numpy as jnp
from jax import lax
from jax.sharding import Mesh
from jax.sharding import PartitionSpec as P

HEAD_DIM = 128
TP = ("tp_0", "tp_1")


def swapped(array, axis, distance):
    return lax.ppermute(array, axis, [(i, i ^ 1 << distance) for i in range(lax.axis_size(axis))])


def from_everyone(array, axis):
    copies = jnp.broadcast_to(array, (lax.axis_size(axis), *array.shape))
    return lax.all_to_all(copies, axis, split_axis=0, concat_axis=0, tiled=True)


def in_order(pieces, dim):
    pieces = jnp.moveaxis(pieces, 0, dim)
    shape = pieces.shape
    return pieces.reshape(*shape[:dim], shape[dim] * shape[dim + 1], *shape[dim + 2 :])


def gather_directly(array, axis, dim):
    pieces = from_everyone(array, axis)
    return in_order(pieces, dim)


def sent_together(arrays, axis, split_dim, concat_dim, along):
    columns = [a.reshape(*a.shape[:along], -1) for a in arrays]
    both = jnp.concatenate(columns, axis=along)
    whole, at, done = (
        lax.all_to_all(both, axis, split_axis=split_dim, concat_axis=concat_dim, tiled=True),
        0,
        [],
    )
    for a, column in zip(arrays, columns):
        slab = whole[..., at : at + column.shape[along]]
        done.append(slab.reshape(*slab.shape[:along], *a.shape[along:]))
        at += column.shape[along]
    return tuple(done)


def sum_by_axis(terms, axes):
    total = terms.astype(jnp.bfloat16)
    for axis in axes:
        total = lax.psum_scatter(total, axis, scatter_dimension=0, tiled=True)
    return total.astype(jnp.float32)


def rotate(values, positions):
    half = values.shape[-1] // 2
    freqs = 500000.0 ** (-jnp.arange(half, dtype=jnp.float32) * 2.0 / values.shape[-1])
    angles = positions.astype(jnp.float32)[..., None] * freqs
    cosine = jnp.cos(angles)
    sine = jnp.sin(angles)
    first = values[..., :half]
    second = values[..., half:]
    return jnp.concatenate([first * cosine - second * sine, second * cosine + first * sine], -1)


def absorb(state, queries, keys, values, key_start, query_start, heads):
    count = keys.shape[0]
    block = math.gcd(count, 1024)
    steps = count // block
    width = keys.shape[1]
    scale = 1.0 / math.sqrt(width)
    query_pos = query_start + jnp.arange(queries.shape[0], dtype=jnp.int32) // heads

    def visit(carry, item):
        best, total, summed = carry
        key_block, value_block, index = item
        scores = (
            lax.dot_general(
                queries, key_block, (((1,), (1,)), ((), ())), preferred_element_type=jnp.float32
            )
            * scale
        )
        if key_start is not None:
            key_pos = key_start + index * block + jnp.arange(block, dtype=jnp.int32)
            scores = jnp.where(key_pos[None, :] <= query_pos[:, None], scores, -1e30)
        top = jnp.maximum(best, jnp.max(scores, axis=1))
        factor = jnp.exp(best - top)
        weights = jnp.exp(scores - top[:, None])
        total = total * factor + jnp.sum(weights, axis=1)
        summed = summed * factor[:, None] + jnp.dot(
            weights.astype(jnp.bfloat16), value_block, preferred_element_type=jnp.float32
        )
        return ((top, total, summed), None)

    result, unused = lax.scan(
        visit,
        state,
        (
            keys.reshape(steps, block, width),
            values.reshape(steps, block, width),
            jnp.arange(steps, dtype=jnp.int32),
        ),
    )
    return result


def body(hidden_states, norm_gain, w_query, w_key, w_value, cache, w_out):
    rows = hidden_states.shape[0]
    groups = lax.axis_size("grp")
    group = lax.axis_index("grp")
    parity = lax.axis_index(TP) % 2
    whole = lax.all_gather(hidden_states, TP, axis=1, tiled=True).astype(jnp.float32)
    normed = (
        whole * lax.rsqrt(jnp.mean(whole * whole, axis=1, keepdims=True) + 1e-05) * norm_gain
    ).astype(jnp.bfloat16)
    prefix = cache.shape[0] * groups
    first = group * rows
    positions = prefix + first + jnp.arange(rows, dtype=jnp.int32)
    heads = w_query.shape[1] // HEAD_DIM
    lanes = rows * heads
    query = jnp.dot(normed, w_query, preferred_element_type=jnp.float32).reshape(
        rows, heads, HEAD_DIM
    )
    query = rotate(query, positions[:, None]).astype(jnp.bfloat16).reshape(lanes, HEAD_DIM)
    key_part = jnp.dot(normed, w_key, preferred_element_type=jnp.float32)
    value_part = jnp.dot(normed, w_value, preferred_element_type=jnp.float32)
    partner_cache = swapped(cache, TP, 0)
    cache_key = jnp.where(parity == 0, cache, partner_cache)
    cache_value = jnp.where(parity == 0, partner_cache, cache)
    partner_key, partner_value = (
        swapped(key_part.astype(jnp.bfloat16), TP, 0).astype(key_part.dtype),
        swapped(value_part.astype(jnp.bfloat16), TP, 0).astype(value_part.dtype),
    )
    key_full = jnp.where(
        parity == 0,
        jnp.concatenate([key_part, partner_key], 1),
        jnp.concatenate([partner_key, key_part], 1),
    )
    value_full = jnp.where(
        parity == 0,
        jnp.concatenate([value_part, partner_value], 1),
        jnp.concatenate([partner_value, value_part], 1),
    )
    key_new = rotate(key_full, positions).astype(jnp.bfloat16)
    value_new = value_full.astype(jnp.bfloat16)
    start_state = (
        jnp.full((lanes,), -1e30, jnp.float32),
        jnp.zeros((lanes,), jnp.float32),
        jnp.zeros((lanes, HEAD_DIM), jnp.float32),
    )
    every = gather_directly(query, "grp", 0).reshape(groups, lanes, HEAD_DIM)

    def serve(item):
        block_queries, block_index = item
        state = absorb(
            start_state, block_queries, cache_key, cache_value, None, block_index * rows, heads
        )
        return absorb(state, block_queries, key_new, value_new, first, block_index * rows, heads)

    best, total, summed = lax.map(serve, (every, jnp.arange(groups, dtype=jnp.int32)))
    summed, best, total = tuple(
        (
            part.astype(jnp.float32)
            for part in sent_together(
                (
                    summed.astype(jnp.bfloat16),
                    best.astype(jnp.bfloat16),
                    total.astype(jnp.bfloat16),
                ),
                "grp",
                0,
                0,
                2,
            )
        )
    )
    top = jnp.max(best, axis=0)
    factor = jnp.exp(best - top[None, :])
    attended = (
        jnp.sum(summed * factor[:, :, None], axis=0) / jnp.sum(total * factor, axis=0)[:, None]
    )
    attended = attended.astype(jnp.bfloat16).reshape(rows, heads * HEAD_DIM)
    mixed = sum_by_axis(
        lax.dot_general(
            w_out, attended, (((0,), (1,)), ((), ())), preferred_element_type=jnp.float32
        ),
        TP,
    )
    return mixed.T.astype(jnp.bfloat16)


def solution(mesh):
    finer = Mesh(mesh.devices.reshape(mesh.shape["grp"], 4, 4), ("grp", "tp_0", "tp_1"))
    in_specs = (P("grp", TP), P(), P(None, TP), P(None, TP), P(None, TP), P("grp", TP), P(TP, None))
    out_specs = P("grp", TP)
    return jax.shard_map(body, mesh=finer, in_specs=in_specs, out_specs=out_specs, check_vma=False)
```

profile of v0, /device:TPU:0, one launch (start us, length us, event | category | flops | bytes accessed | tf_op | source)
XLA Modules:
  0.0 305.9 jit_solution(13559694169984585403)
XLA Ops:
  7.3 62.4 %all-gather.2.cloned.1.call-done = bf16[256,8192]{1,0:T(8,128)(2,1)} async-done(((bf16[256,512]{1,0:T(8,128)(2,1)}), bf16[256,8192]{1,0:T(8,128)(2,1)}) %all-gather.2.cloned.1.call-update) | async-done | bytes 4194320 | tf_op jit(solution)/shard_map/all_gather | solution.py:111
  69.7 3.3 %fusion.29 = f32[256]{0:T(256)S(1)} fusion(bf16[256,8192]{1,0:T(8,128)(2,1)} %all-gather.2.cloned.1.call-done), kind=kLoop, calls=%fused_computation.46 | loop fusion | flops 6291200 | bytes 4195328 | tf_op jit(solution)/shard_map/reduce_sum | solution.py:113
  73.2 1.5 fusion.49
  76.5 2.4 fusion.45
  80.3 1.7 broadcast_in_dim.80
  82.0 4.3 %all-to-all-start = ((bf16[8,1024,128]{2,1,0:T(8,128)(2,1)}), bf16[8,1024,128]{2,1,0:T(8,128)(2,1)}, u32[]{:S(2)}, u32[]{:S(2)}) async-start(bf16[8,1024,128]{2,1,0:T(8,128)(2,1)} %broadcast_in_dim.80), calls=%async_computation | async-start | bytes 4194304 | tf_op jit(solution)/shard_map/all_to_all | solution.py:18
  86.4 1.3 collective-permute-start
  87.7 3.9 %fusion.41 = bf16[256,64]{0,1:T(8,128)(2,1)S(1)} fusion(bf16[8192,64]{0,1:T(8,128)(2,1)} %param.15, bf16[256,8192]{1,0:T(8,128)(2,1)} %all-gather.2.cloned.1.call-done, f32[8192]{0:T(1024)S(1)} %copy-done.4, f32[256]{0:T(256)S(1)} %add_rsqrt_fusion), kind=kOutput, calls=%fused_computation.81 | convolution fusion | flops 276824064 | bytes 5309440 | tf_op jit(solution)/shard_map/dot_general | solution.py:125
  92.7 8.3 %collective-permute-done = bf16[2048,128]{1,0:T(8,128)(2,1)S(1)} collective-permute-done((bf16[2048,128]{1,0:T(8,128)(2,1)S(1)}, bf16[2048,128]{1,0:T(8,128)(2,1)S(1)}, u32[]{:S(2)}, u32[]{:S(2)}) %collective-permute-start) | collective-permute-done | bytes 524320 | tf_op jit(solution)/shard_map/ppermute | solution.py:13
  101.7 11.9 %all-to-all-done = bf16[8,1024,128]{2,1,0:T(8,128)(2,1)} async-done(((bf16[8,1024,128]{2,1,0:T(8,128)(2,1)}), bf16[8,1024,128]{2,1,0:T(8,128)(2,1)}, u32[]{:S(2)}, u32[]{:S(2)}) %all-to-all-start) | async-done | bytes 2097184 | tf_op jit(solution)/shard_map/all_to_all | solution.py:18
  113.6 73.2 %while.47 = (s32[]{:T(128)}, bf16[8,1024]{1,0:T(8,128)(2,1)S(1)}, bf16[8,1024]{1,0:T(8,128)(2,1)S(1)}, bf16[8,1024,128]{1,2,0:T(8,128)(2,1)}, bf16[2048,128]{1,0...) while((s32[]{:T(128)}, bf16[8,1024]{1,0:T(8,128)(2,1)S(1)}, ...), condition=%wide.region_8.9_spmd, body=%wide.region_1.8_spmd.sunk | while | flops 682377472 | bytes 20466068 | solution.py:159
  115.8 5.0 %while.48 = (s32[]{:T(128)}, f32[1024]{0:T(1024)S(1)}, f32[1024]{0:T(1024)S(1)}, f32[1024,128]{1,0:T(8,128)S(1)}, bf16[2,1024,128]{2,1,0:T(8,128)(2,1)S(1)}, /*i...) while((s32[]{:T(128)}, f32[1024]{0:T(1024)S(1)}, ...), condition=%wide.region_5.5_spmd.clone, body=%wide.region_2.4_spmd.clone.sunk | while | flops 545657856 | bytes 14483577 | solution.py:94
  124.9 5.0 %while.48 = (s32[]{:T(128)}, f32[1024]{0:T(1024)S(1)}, f32[1024]{0:T(1024)S(1)}, f32[1024,128]{1,0:T(8,128)S(1)}, bf16[2,1024,128]{2,1,0:T(8,128)(2,1)S(1)}, /*i...) while((s32[]{:T(128)}, f32[1024]{0:T(1024)S(1)}, ...), condition=%wide.region_5.5_spmd.clone, body=%wide.region_2.4_spmd.clone.sunk | while | flops 545657856 | bytes 14483577 | solution.py:94
  134.1 5.0 %while.48 = (s32[]{:T(128)}, f32[1024]{0:T(1024)S(1)}, f32[1024]{0:T(1024)S(1)}, f32[1024,128]{1,0:T(8,128)S(1)}, bf16[2,1024,128]{2,1,0:T(8,128)(2,1)S(1)}, /*i...) while((s32[]{:T(128)}, f32[1024]{0:T(1024)S(1)}, ...), condition=%wide.region_5.5_spmd.clone, body=%wide.region_2.4_spmd.clone.sunk | while | flops 545657856 | bytes 14483577 | solution.py:94
  143.2 5.0 %while.48 = (s32[]{:T(128)}, f32[1024]{0:T(1024)S(1)}, f32[1024]{0:T(1024)S(1)}, f32[1024,128]{1,0:T(8,128)S(1)}, bf16[2,1024,128]{2,1,0:T(8,128)(2,1)S(1)}, /*i...) while((s32[]{:T(128)}, f32[1024]{0:T(1024)S(1)}, ...), condition=%wide.region_5.5_spmd.clone, body=%wide.region_2.4_spmd.clone.sunk | while | flops 545657856 | bytes 14483577 | solution.py:94
  152.4 5.0 %while.48 = (s32[]{:T(128)}, f32[1024]{0:T(1024)S(1)}, f32[1024]{0:T(1024)S(1)}, f32[1024,128]{1,0:T(8,128)S(1)}, bf16[2,1024,128]{2,1,0:T(8,128)(2,1)S(1)}, /*i...) while((s32[]{:T(128)}, f32[1024]{0:T(1024)S(1)}, ...), condition=%wide.region_5.5_spmd.clone, body=%wide.region_2.4_spmd.clone.sunk | while | flops 545657856 | bytes 14483577 | solution.py:94
  161.5 5.0 %while.48 = (s32[]{:T(128)}, f32[1024]{0:T(1024)S(1)}, f32[1024]{0:T(1024)S(1)}, f32[1024,128]{1,0:T(8,128)S(1)}, bf16[2,1024,128]{2,1,0:T(8,128)(2,1)S(1)}, /*i...) while((s32[]{:T(128)}, f32[1024]{0:T(1024)S(1)}, ...), condition=%wide.region_5.5_spmd.clone, body=%wide.region_2.4_spmd.clone.sunk | while | flops 545657856 | bytes 14483577 | solution.py:94
  170.7 5.0 %while.48 = (s32[]{:T(128)}, f32[1024]{0:T(1024)S(1)}, f32[1024]{0:T(1024)S(1)}, f32[1024,128]{1,0:T(8,128)S(1)}, bf16[2,1024,128]{2,1,0:T(8,128)(2,1)S(1)}, /*i...) while((s32[]{:T(128)}, f32[1024]{0:T(1024)S(1)}, ...), condition=%wide.region_5.5_spmd.clone, body=%wide.region_2.4_spmd.clone.sunk | while | flops 545657856 | bytes 14483577 | solution.py:94
  179.8 5.0 %while.48 = (s32[]{:T(128)}, f32[1024]{0:T(1024)S(1)}, f32[1024]{0:T(1024)S(1)}, f32[1024,128]{1,0:T(8,128)S(1)}, bf16[2,1024,128]{2,1,0:T(8,128)(2,1)S(1)}, /*i...) while((s32[]{:T(128)}, f32[1024]{0:T(1024)S(1)}, ...), condition=%wide.region_5.5_spmd.clone, body=%wide.region_2.4_spmd.clone.sunk | while | flops 545657856 | bytes 14483577 | solution.py:94
  186.8 1.9 pad_maximum_fusion
  188.7 31.3 %all_to_all.10 = bf16[8,1024,130]{1,2,0:T(8,128)(2,1)S(1)} all-to-all(bf16[8,1024,130]{1,2,0:T(8,128)(2,1)S(1)} %pad_maximum_fusion), channel_id=1, replica_groups=mesh['grp'=8,'tp_0'=4,'tp_1'=4] {'grp'}, dimensions={0} | all-to-all | bytes 4259840 | tf_op jit(solution)/shard_map/all_to_all | solution.py:36
  221.4 7.7 %fusion.28 = bf16[8192,256]{0,1:T(8,128)(2,1)} fusion(bf16[512,8192]{1,0:T(8,128)(2,1)} %param.17, f32[256,512]{1,0:T(8,128)S(1)} %reduce_sum.54, f32[32,8,4,128]{3,2,1,0:T(4,128)S(1)} %bitcast.92), kind=kOutput, calls=%fused_computation.45 | convolution fusion | flops 2149842944 | bytes 13631488 | tf_op jit(solution)/shard_map/dot_general | solution.py:183
  229.2 44.6 %reduce-scatter.3.cloned.1.call-done = bf16[2048,256]{0,1:T(8,128)(2,1)} async-done(((bf16[8192,256]{0,1:T(8,128)(2,1)}), bf16[2048,256]{0,1:T(8,128)(2,1)}) %reduce-scatter.3.cloned.1.call-update) | async-done | bytes 1048592 | tf_op jit(solution)/shard_map/reduce_scatter | solution.py:50
  273.8 25.7 %reduce-scatter.5.cloned.1.call-done = bf16[512,256]{0,1:T(8,128)(2,1)} async-done(((bf16[2048,256]{0,1:T(8,128)(2,1)}), bf16[512,256]{0,1:T(8,128)(2,1)}) %reduce-scatter.5.cloned.1.call-update) | async-done | bytes 262160 | tf_op jit(solution)/shard_map/reduce_scatter | solution.py:50
  (275 shorter events, 74.4 us)
Async XLA Ops:
  6.5 66.4 %copy-start = (bf16[8192,64]{0,1:T(8,128)(2,1)S(1)}, bf16[8192,64]{0,1:T(8,128)(2,1)}, u32[]{:S(2)}) copy-start(bf16[8192,64]{0,1:T(8,128)(2,1)} %param.14) | copy-start | bytes 3145732
  6.5 66.4 %copy-start.4 = (f32[8192]{0:T(1024)S(1)}, f32[8192]{0:T(1024)}, u32[]{:S(2)}) copy-start(f32[8192]{0:T(1024)} %param.12) | copy-start | bytes 98308
  6.5 63.2 %all-gather.2.cloned.1.call-start = ((), (), s32[]{:S(2)}) async-start(), calls=%async_computation.4 | async-start | bytes 4456448 | tf_op jit(solution)/shard_map/all_gather | solution.py:111
  69.7 3.4 %copy-start.1 = (bf16[256,8192]{1,0:T(8,128)(2,1)S(1)}, bf16[256,8192]{1,0:T(8,128)(2,1)}, u32[]{:S(2)}) copy-start(bf16[256,8192]{1,0:T(8,128)(2,1)} %all-gather.2.cloned.1.call-done) | copy-start | bytes 12582916
  73.1 3.4 %copy-start.3 = (bf16[8192,512]{1,0:T(8,128)(2,1)S(1)}, bf16[8192,512]{1,0:T(8,128)(2,1)}, u32[]{:S(2)}) copy-start(bf16[8192,512]{1,0:T(8,128)(2,1)} %param.13) | copy-start | bytes 25165828
  74.7 4.4 %collective-permute-start.1 = (bf16[256,64]{0,1:T(8,128)(2,1)S(1)}, bf16[256,64]{0,1:T(8,128)(2,1)S(1)}, u32[]{:S(2)}, u32[]{:S(2)}) collective-permute-start(bf16[256,64]{0,1:T(8,128)(2,1)S(1)} %get-tuple-element.383), channel_id=1, source_target_pairs={{0,1},{1,0},{2,3},{3,2},{4,5},{5,4},{6,7},{7,6},{8,9},{9,8},{10,11... | collective-permute-start | bytes 98312 | tf_op jit(solution)/shard_map/ppermute | solution.py:13
  79.7 6.7 %copy-start.2 = (bf16[2048,128]{1,0:T(8,128)(2,1)S(1)}, bf16[2048,128]{1,0:T(8,128)(2,1)}, u32[]{:S(2)}) copy-start(bf16[2048,128]{1,0:T(8,128)(2,1)} %param.16) | copy-start | bytes 1572868
  82.0 31.6 %all-to-all-start = ((bf16[8,1024,128]{2,1,0:T(8,128)(2,1)}), bf16[8,1024,128]{2,1,0:T(8,128)(2,1)}, u32[]{:S(2)}, u32[]{:S(2)}) async-start(bf16[8,1024,128]{2,1,0:T(8,128)(2,1)} %broadcast_in_dim.80), calls=%async_computation | async-start | bytes 4194304 | tf_op jit(solution)/shard_map/all_to_all | solution.py:18
  86.4 187.4 %reduce-scatter.3.cloned.1.call-start = ((), (), s32[]{:S(2)}) async-start(), calls=%async_computation.5 | async-start | bytes 5242880 | tf_op jit(solution)/shard_map/reduce_scatter | solution.py:50
  86.4 14.6 %collective-permute-start = (bf16[2048,128]{1,0:T(8,128)(2,1)S(1)}, bf16[2048,128]{1,0:T(8,128)(2,1)S(1)}, u32[]{:S(2)}, u32[]{:S(2)}) collective-permute-start(bf16[2048,128]{1,0:T(8,128)(2,1)S(1)} %copy-done.2), channel_id=1, source_target_pairs={{0,1},{1,0},{2,3},{3,2},{4,5},{5,4},{6,7},{7,6},{8,9},{9,8},{10,11... | collective-permute-start | bytes 1572872 | tf_op jit(solution)/shard_map/ppermute | solution.py:13
  91.6 9.8 %collective-permute-start.2 = (bf16[256,64]{0,1:T(8,128)(2,1)S(1)}, bf16[256,64]{0,1:T(8,128)(2,1)S(1)}, u32[]{:S(2)}, u32[]{:S(2)}) collective-permute-start(bf16[256,64]{0,1:T(8,128)(2,1)S(1)} %fusion.41), channel_id=1, source_target_pairs={{0,1},{1,0},{2,3},{3,2},{4,5},{5,4},{6,7},{7,6},{8,9},{9,8},{10,11... | collective-permute-start | bytes 98312 | tf_op jit(solution)/shard_map/ppermute | solution.py:13
  229.1 70.3 %reduce-scatter.5.cloned.1.call-start = ((), (), s32[]{:S(2)}) async-start(), calls=%async_computation.6 | async-start | bytes 1310720 | tf_op jit(solution)/shard_map/reduce_scatter | solution.py:50
Sparse Core Ops, SparseCore 0:
  9.5 60.1 all-gather.1
  229.2 44.4 reduce-scatter.2
  276.3 23.0 reduce-scatter.4
where the time goes:
time: 307 us; the launch traced here: 306 us
  waiting for transfers between devices  154 us (50%)
  matrix products  48.3 us (16%)
  blocking collectives  31.3 us (10%)
  local copies, waits for them, and re-layouts  24.4 us (8%)
  other arithmetic  20.5 us (7%)
  between operations  13.4 us (4%)
  starting transfers between devices  8.07 us (3%)
  loops' own time  6.1 us (2%)
    reduce_scatter x2, waiting for transfers between devices, sum_by_axis(): total = lax.psum_scatter(total, axis, scatter_dimension=0, tiled=True)  70.2 us
    all_gather x1, waiting for transfers between devices, body(): lax.all_gather(hidden_states, TP, axis=1, tiled=True).astype(jnp.float32)  62.4 us
    all_to_all x1, blocking collectives, sent_together(): lax.all_to_all(both, axis, split_axis=split_dim, concat_axis=concat_dim,...  31.3 us
    dot_general x24, matrix products, visit(): jnp.dot(weights.astype(jnp.bfloat16), value_block, preferred_element_type...  18.8 us
    dot_general x24, matrix products, visit(): lax.dot_general(queries, key_block, (((1,), (1,)), ((), ())), preferred_e...  14 us
    reduce_sum x24, other arithmetic, visit(): total = total * factor + jnp.sum(weights, axis=1)  13.1 us
    all_to_all x1, waiting for transfers between devices, from_everyone(): return lax.all_to_all(copies, axis, split_axis=0, concat_axis=0, tiled=True)  11.9 us
    ppermute x3, waiting for transfers between devices, swapped(): lax.ppermute(array, axis, [(i, i ^ 1 << distance) for i in range(lax.axis...  8.59 us
  transfers between devices with their start and end apart: 7, of which 6 were waited for; matrix products, arithmetic and copies ran while one was open for 2% of the time, Pallas kernels for 0%

commit v1 on v0

--- a/solution.py
+++ b/solution.py
@@ -108,7 +108,9 @@
     groups = lax.axis_size("grp")
     group = lax.axis_index("grp")
     parity = lax.axis_index(TP) % 2
-    whole = lax.all_gather(hidden_states, TP, axis=1, tiled=True).astype(jnp.float32)
+    whole = jnp.concatenate(
+        lax.all_to_all(jnp.stack([hidden_states] * lax.axis_size(TP)), TP, 0, 0), axis=1
+    ).astype(jnp.float32)
     normed = (
         whole * lax.rsqrt(jnp.mean(whole * whole, axis=1, keepdims=True) + 1e-05) * norm_gain
     ).astype(jnp.bfloat16)

time: 307 us -> 402 us (1.31)
  other arithmetic: 20.5 us -> 60.3 us
  matrix products: 48.3 us -> 77.6 us
  local copies, waits for them, and re-layouts: 24.4 us -> 52.9 us
  waiting for transfers between devices: 154 us -> 143 us
  starting transfers between devices: 8.07 us -> 15.2 us
    all_gather x1 -> x0, waiting for transfers between devices: 62.4 us -> none  [body(): lax.all_gather(hidden_states, TP, axis=1, tiled=True).astype(jnp.float32)]
    all_to_all x0 -> x1, waiting for transfers between devices: none -> 51.4 us  [body(): lax.all_to_all(jnp.stack([hidden_states] * lax.axis_size(TP)), TP, 0, 0)]
    reduce_sum x24, other arithmetic: 13.1 us -> 50.6 us  [visit(): total = total * factor + jnp.sum(weights, axis=1)]
    dot_general x24, matrix products: 14 us -> 44.9 us  [visit(): lax.dot_general(queries, key_block, (((1,), (1,)), ((), ())), preferred_e...]
    dot_general x0 -> x1, local copies, waits for them, and re-layouts: none -> 11.7 us  [body(): jnp.dot(normed, w_query, preferred_element_type=jnp.float32)]
    all_to_all x0 -> x1, starting transfers between devices: none -> 8.31 us  [body(): lax.all_to_all(jnp.stack([hidden_states] * lax.axis_size(TP)), TP, 0, 0)]
    all_to_all x0 -> x1, local copies, waits for them, and re-layouts: none -> 6.36 us  [body(): lax.all_to_all(jnp.stack([hidden_states] * lax.axis_size(TP)), TP, 0, 0)]
    while x16 -> x48, local copies, waits for them, and re-layouts: 0.04 us -> 5.76 us
  transfers between devices with their start and end apart: 7 -> 7, of which waited for: 6 -> 6; matrix products, arithmetic and copies ran while one was open for 2% -> 5% of each run, Pallas kernels for 0% -> 0%
where the time goes in v1:
time: 402 us; the launch traced here: 401 us
  waiting for transfers between devices  143 us (36%)
  matrix products  77.6 us (19%)
  other arithmetic  60.3 us (15%)
  local copies, waits for them, and re-layouts  52.9 us (13%)
  blocking collectives  31.3 us (8%)
  starting transfers between devices  15.2 us (4%)
  between operations  13.8 us (3%)
  loops' own time  6.96 us (2%)
    reduce_scatter x2, waiting for transfers between devices, sum_by_axis(): total = lax.psum_scatter(total, axis, scatter_dimension=0, tiled=True)  69.8 us
    all_to_all x1, waiting for transfers between devices, body(): lax.all_to_all(jnp.stack([hidden_states] * lax.axis_size(TP)), TP, 0, 0)  51.4 us
    reduce_sum x24, other arithmetic, visit(): total = total * factor + jnp.sum(weights, axis=1)  50.6 us
    dot_general x24, matrix products, visit(): lax.dot_general(queries, key_block, (((1,), (1,)), ((), ())), preferred_e...  44.9 us
    all_to_all x1, blocking collectives, sent_together(): lax.all_to_all(both, axis, split_axis=split_dim, concat_axis=concat_dim,...  31.3 us
    dot_general x24, matrix products, visit(): jnp.dot(weights.astype(jnp.bfloat16), value_block, preferred_element_type...  18.8 us
    all_to_all x1, waiting for transfers between devices, from_everyone(): return lax.all_to_all(copies, axis, split_axis=0, concat_axis=0, tiled=True)  11.9 us
    dot_general x1, local copies, waits for them, and re-layouts, body(): jnp.dot(normed, w_query, preferred_element_type=jnp.float32)  11.7 us
  transfers between devices with their start and end apart: 7, of which 6 were waited for; matrix products, arithmetic and copies ran while one was open for 5% of the time, Pallas kernels for 0%

profile of v1, /device:TPU:0, one launch (start us, length us, event | category | flops | bytes accessed | tf_op | source)
XLA Modules:
  0.0 400.8 jit_solution(12619312428238322808)
XLA Ops:
  6.5 3.4 stack.2
  9.9 8.3 %all-to-all-start = ((bf16[16,256,512]{2,1,0:T(8,128)(2,1)}), bf16[16,256,512]{2,1,0:T(8,128)(2,1)}, u32[]{:S(2)}, u32[]{:S(2)}) async-start(bf16[16,256,512]{2,1,0:T(8,128)(2,1)} %stack.2), calls=%async_computation | async-start | bytes 8388608 | tf_op jit(solution)/shard_map/all_to_all | solution.py:112
  18.3 11.7 %copy.45 = bf16[512,8192]{1,0:T(8,128)(2,1)} copy(bf16[512,8192]{0,1:T(8,128)(2,1)} %bitcast.107) | data formatting | bytes 16777216 | tf_op jit(solution)/shard_map/dot_general | solution.py:122
  30.1 51.4 %all-to-all-done = bf16[16,256,512]{2,1,0:T(8,128)(2,1)} async-done(((bf16[16,256,512]{2,1,0:T(8,128)(2,1)}), bf16[16,256,512]{2,1,0:T(8,128)(2,1)}, u32[]{:S(2)}, u32[]{:S(2)}) %all-to-all-start) | async-done | bytes 4194336 | tf_op jit(solution)/shard_map/all_to_all | solution.py:112
  81.5 6.4 %copy.29 = bf16[16,256,512]{1,2,0:T(8,128)(2,1)} copy(bf16[16,256,512]{2,1,0:T(8,128)(2,1)} %all-to-all-done) | data formatting | bytes 8388608 | tf_op jit(solution)/shard_map/all_to_all | solution.py:112
  87.8 3.5 multiply_reduce_fusion.1
  101.5 4.4 %all-to-all-start.1 = ((bf16[8,1024,128]{2,1,0:T(8,128)(2,1)}), bf16[8,1024,128]{2,1,0:T(8,128)(2,1)}, u32[]{:S(2)}, u32[]{:S(2)}) async-start(bf16[8,1024,128]{2,1,0:T(8,128)(2,1)} %broadcast_in_dim.80), calls=%async_computation.1 | async-start | bytes 4194304 | tf_op jit(solution)/shard_map/all_to_all | solution.py:18
  111.3 9.3 %collective-permute-done = bf16[2048,128]{1,0:T(8,128)(2,1)S(1)} collective-permute-done((bf16[2048,128]{1,0:T(8,128)(2,1)S(1)}, bf16[2048,128]{1,0:T(8,128)(2,1)S(1)}, u32[]{:S(2)}, u32[]{:S(2)}) %collective-permute-start) | collective-permute-done | bytes 524320 | tf_op jit(solution)/shard_map/ppermute | solution.py:13
  121.2 11.9 %all-to-all-done.1 = bf16[8,1024,128]{2,1,0:T(8,128)(2,1)} async-done(((bf16[8,1024,128]{2,1,0:T(8,128)(2,1)}), bf16[8,1024,128]{2,1,0:T(8,128)(2,1)}, u32[]{:S(2)}, u32[]{:S(2)}) %all-to-all-start.1) | async-done | bytes 2097184 | tf_op jit(solution)/shard_map/all_to_all | solution.py:18
  133.1 148.5 %while.47 = (s32[]{:T(128)}, bf16[8,1024]{1,0:T(8,128)(2,1)S(1)}, bf16[8,1024]{1,0:T(8,128)(2,1)S(1)}, bf16[8,1024,128]{1,2,0:T(8,128)(2,1)}, bf16[2048,128]{1,0...) while((s32[]{:T(128)}, bf16[8,1024]{1,0:T(8,128)(2,1)S(1)}, ...), condition=%wide.region_8.9_spmd, body=%wide.region_1.8_spmd.sunk | while | flops 682377472 | bytes 37243804 | solution.py:161
  135.8 14.2 %while.48 = (s32[]{:T(128)}, f32[1024]{0:T(1024)S(1)}, f32[1024]{0:T(1024)S(1)}, f32[1024,128]{1,0:T(8,128)S(1)}, bf16[2,1024,128]{2,1,0:T(8,128)(2,1)S(1)}, /*i...) while((s32[]{:T(128)}, f32[1024]{0:T(1024)S(1)}, ...), condition=%wide.region_5.5_spmd.clone, body=%wide.region_2.4_spmd.clone.sunk | while | flops 545657856 | bytes 31260812 | solution.py:94
  138.5 3.1 fusion.81
  145.6 3.1 fusion.81
  154.4 14.2 %while.48 = (s32[]{:T(128)}, f32[1024]{0:T(1024)S(1)}, f32[1024]{0:T(1024)S(1)}, f32[1024,128]{1,0:T(8,128)S(1)}, bf16[2,1024,128]{2,1,0:T(8,128)(2,1)S(1)}, /*i...) while((s32[]{:T(128)}, f32[1024]{0:T(1024)S(1)}, ...), condition=%wide.region_5.5_spmd.clone, body=%wide.region_2.4_spmd.clone.sunk | while | flops 545657856 | bytes 31260812 | solution.py:94
  172.9 14.2 %while.48 = (s32[]{:T(128)}, f32[1024]{0:T(1024)S(1)}, f32[1024]{0:T(1024)S(1)}, f32[1024,128]{1,0:T(8,128)S(1)}, bf16[2,1024,128]{2,1,0:T(8,128)(2,1)S(1)}, /*i...) while((s32[]{:T(128)}, f32[1024]{0:T(1024)S(1)}, ...), condition=%wide.region_5.5_spmd.clone, body=%wide.region_2.4_spmd.clone.sunk | while | flops 545657856 | bytes 31260812 | solution.py:94
  191.5 14.2 %while.48 = (s32[]{:T(128)}, f32[1024]{0:T(1024)S(1)}, f32[1024]{0:T(1024)S(1)}, f32[1024,128]{1,0:T(8,128)S(1)}, bf16[2,1024,128]{2,1,0:T(8,128)(2,1)S(1)}, /*i...) while((s32[]{:T(128)}, f32[1024]{0:T(1024)S(1)}, ...), condition=%wide.region_5.5_spmd.clone, body=%wide.region_2.4_spmd.clone.sunk | while | flops 545657856 | bytes 31260812 | solution.py:94
  210.0 14.2 %while.48 = (s32[]{:T(128)}, f32[1024]{0:T(1024)S(1)}, f32[1024]{0:T(1024)S(1)}, f32[1024,128]{1,0:T(8,128)S(1)}, bf16[2,1024,128]{2,1,0:T(8,128)(2,1)S(1)}, /*i...) while((s32[]{:T(128)}, f32[1024]{0:T(1024)S(1)}, ...), condition=%wide.region_5.5_spmd.clone, body=%wide.region_2.4_spmd.clone.sunk | while | flops 545657856 | bytes 31260812 | solution.py:94
  228.6 14.2 %while.48 = (s32[]{:T(128)}, f32[1024]{0:T(1024)S(1)}, f32[1024]{0:T(1024)S(1)}, f32[1024,128]{1,0:T(8,128)S(1)}, bf16[2,1024,128]{2,1,0:T(8,128)(2,1)S(1)}, /*i...) while((s32[]{:T(128)}, f32[1024]{0:T(1024)S(1)}, ...), condition=%wide.region_5.5_spmd.clone, body=%wide.region_2.4_spmd.clone.sunk | while | flops 545657856 | bytes 31260812 | solution.py:94
  247.1 14.2 %while.48 = (s32[]{:T(128)}, f32[1024]{0:T(1024)S(1)}, f32[1024]{0:T(1024)S(1)}, f32[1024,128]{1,0:T(8,128)S(1)}, bf16[2,1024,128]{2,1,0:T(8,128)(2,1)S(1)}, /*i...) while((s32[]{:T(128)}, f32[1024]{0:T(1024)S(1)}, ...), condition=%wide.region_5.5_spmd.clone, body=%wide.region_2.4_spmd.clone.sunk | while | flops 545657856 | bytes 31260812 | solution.py:94
  265.7 14.2 %while.48 = (s32[]{:T(128)}, f32[1024]{0:T(1024)S(1)}, f32[1024]{0:T(1024)S(1)}, f32[1024,128]{1,0:T(8,128)S(1)}, bf16[2,1024,128]{2,1,0:T(8,128)(2,1)S(1)}, /*i...) while((s32[]{:T(128)}, f32[1024]{0:T(1024)S(1)}, ...), condition=%wide.region_5.5_spmd.clone, body=%wide.region_2.4_spmd.clone.sunk | while | flops 545657856 | bytes 31260812 | solution.py:94
  283.6 31.3 %all_to_all.15 = bf16[8,1024,130]{1,2,0:T(8,128)(2,1)S(1)} all-to-all(bf16[8,1024,130]{1,2,0:T(8,128)(2,1)S(1)} %pad_maximum_fusion), channel_id=1, replica_groups=mesh['grp'=8,'tp_0'=4,'tp_1'=4] {'grp'}, dimensions={0} | all-to-all | bytes 4259840 | tf_op jit(solution)/shard_map/all_to_all | solution.py:36
  316.2 7.8 %fusion.28 = bf16[8192,256]{0,1:T(8,128)(2,1)} fusion(bf16[512,8192]{1,0:T(8,128)(2,1)} %param.17, f32[256,512]{1,0:T(8,128)S(1)} %reduce_sum.54, f32[32,8,4,128]{3,2,1,0:T(4,128)S(1)} %bitcast.115), kind=kOutput, calls=%fused_computation.43 | convolution fusion | flops 2149842944 | bytes 13631488 | tf_op jit(solution)/shard_map/dot_general | solution.py:185
  324.1 44.2 %reduce-scatter.3.cloned.1.call-done = bf16[2048,256]{0,1:T(8,128)(2,1)} async-done(((bf16[8192,256]{0,1:T(8,128)(2,1)}), bf16[2048,256]{0,1:T(8,128)(2,1)}) %reduce-scatter.3.cloned.1.call-update) | async-done | bytes 1048592 | tf_op jit(solution)/shard_map/reduce_scatter | solution.py:50
  368.3 25.6 %reduce-scatter.5.cloned.1.call-done = bf16[512,256]{0,1:T(8,128)(2,1)} async-done(((bf16[2048,256]{0,1:T(8,128)(2,1)}), bf16[512,256]{0,1:T(8,128)(2,1)}) %reduce-scatter.5.cloned.1.call-update) | async-done | bytes 262160 | tf_op jit(solution)/shard_map/reduce_scatter | solution.py:50
  (320 shorter events, 154.8 us)
Async XLA Ops:
  6.5 86.0 %copy-start = (bf16[8192,64]{0,1:T(8,128)(2,1)S(1)}, bf16[8192,64]{0,1:T(8,128)(2,1)}, u32[]{:S(2)}) copy-start(bf16[8192,64]{0,1:T(8,128)(2,1)} %param.14) | copy-start | bytes 3145732
  9.9 8.3 %copy-start.7 = (f32[8192]{0:T(1024)S(1)}, f32[8192]{0:T(1024)}, u32[]{:S(2)}) copy-start(f32[8192]{0:T(1024)} %param.12) | copy-start | bytes 98308
  9.9 71.5 %all-to-all-start = ((bf16[16,256,512]{2,1,0:T(8,128)(2,1)}), bf16[16,256,512]{2,1,0:T(8,128)(2,1)}, u32[]{:S(2)}, u32[]{:S(2)}) async-start(bf16[16,256,512]{2,1,0:T(8,128)(2,1)} %stack.2), calls=%async_computation | async-start | bytes 8388608 | tf_op jit(solution)/shard_map/all_to_all | solution.py:112
  87.8 3.5 copy-start.3
  91.3 3.6 slice-start
  92.6 3.9 slice-start.1
  93.4 5.5 %collective-permute-start.1 = (bf16[256,64]{0,1:T(8,128)(2,1)S(1)}, bf16[256,64]{0,1:T(8,128)(2,1)S(1)}, u32[]{:S(2)}, u32[]{:S(2)}) collective-permute-start(bf16[256,64]{0,1:T(8,128)(2,1)S(1)} %get-tuple-element.383), channel_id=1, source_target_pairs={{0,1},{1,0},{2,3},{3,2},{4,5},{5,4},{6,7},{7,6},{8,9},{9,8},{10,11... | collective-permute-start | bytes 98312 | tf_op jit(solution)/shard_map/ppermute | solution.py:13
  99.3 6.6 %copy-start.6 = (bf16[2048,128]{1,0:T(8,128)(2,1)S(1)}, bf16[2048,128]{1,0:T(8,128)(2,1)}, u32[]{:S(2)}) copy-start(bf16[2048,128]{1,0:T(8,128)(2,1)} %param.16) | copy-start | bytes 1572868
  99.3 7.1 %copy-start.5 = (bf16[8192,64]{0,1:T(8,128)(2,1)S(1)}, bf16[8192,64]{0,1:T(8,128)(2,1)}, u32[]{:S(2)}) copy-start(bf16[8192,64]{0,1:T(8,128)(2,1)} %param.15) | copy-start | bytes 3145732
  101.5 31.6 %all-to-all-start.1 = ((bf16[8,1024,128]{2,1,0:T(8,128)(2,1)}), bf16[8,1024,128]{2,1,0:T(8,128)(2,1)}, u32[]{:S(2)}, u32[]{:S(2)}) async-start(bf16[8,1024,128]{2,1,0:T(8,128)(2,1)} %broadcast_in_dim.80), calls=%async_computation.1 | async-start | bytes 4194304 | tf_op jit(solution)/shard_map/all_to_all | solution.py:18
  105.9 262.4 %reduce-scatter.3.cloned.1.call-start = ((), (), s32[]{:S(2)}) async-start(), calls=%async_computation.5 | async-start | bytes 5242880 | tf_op jit(solution)/shard_map/reduce_scatter | solution.py:50
  105.9 14.6 %collective-permute-start = (bf16[2048,128]{1,0:T(8,128)(2,1)S(1)}, bf16[2048,128]{1,0:T(8,128)(2,1)S(1)}, u32[]{:S(2)}, u32[]{:S(2)}) collective-permute-start(bf16[2048,128]{1,0:T(8,128)(2,1)S(1)} %copy-done.6), channel_id=1, source_target_pairs={{0,1},{1,0},{2,3},{3,2},{4,5},{5,4},{6,7},{7,6},{8,9},{9,8},{10,11... | collective-permute-start | bytes 1572872 | tf_op jit(solution)/shard_map/ppermute | solution.py:13
  109.5 11.5 %collective-permute-start.2 = (bf16[256,64]{0,1:T(8,128)(2,1)S(1)}, bf16[256,64]{0,1:T(8,128)(2,1)S(1)}, u32[]{:S(2)}, u32[]{:S(2)}) collective-permute-start(bf16[256,64]{0,1:T(8,128)(2,1)S(1)} %fusion.44), channel_id=1, source_target_pairs={{0,1},{1,0},{2,3},{3,2},{4,5},{5,4},{6,7},{7,6},{8,9},{9,8},{10,11... | collective-permute-start | bytes 98312 | tf_op jit(solution)/shard_map/ppermute | solution.py:13
  145.6 3.4 copy-start.2
  164.1 3.4 copy-start.2
  175.6 3.4 copy-start.2
  212.7 3.4 copy-start.2
  231.3 3.4 copy-start.2
  238.4 3.4 copy-start.2
  256.9 3.4 copy-start.2
  268.4 3.4 copy-start.2
  275.5 3.4 copy-start.2
  316.2 77.7 %copy-start.1 = (bf16[8192,64]{0,1:T(8,128)(2,1)S(1)}, bf16[8192,64]{0,1:T(8,128)(2,1)}, u32[]{:S(2)}) copy-start(bf16[8192,64]{0,1:T(8,128)(2,1)} %param.14) | copy-start | bytes 3145732
  324.0 69.9 %reduce-scatter.5.cloned.1.call-start = ((), (), s32[]{:S(2)}) async-start(), calls=%async_computation.6 | async-start | bytes 1310720 | tf_op jit(solution)/shard_map/reduce_scatter | solution.py:50
  (8 other events, 26.5 us)
Sparse Core Ops, SparseCore 0:
  324.2 44.0 reduce-scatter.2
  370.8 23.0 reduce-scatter.4
